TPU v7x, 256 devices: a whole 4x4x8 slice. The times are simulated.
256 devices in a mesh: fsdp: 32 (over y, x, core), tp: 8 (over z).
Axes of the slice: x: 4, y: 4, z: 8, core: 2. Of those that a mesh axis runs over, the one named last changes fastest.
Arguments:
- learner_flat: bfloat16 [2, 159383552], P(None, ('fsdp', 'tp')), may hold values from -1.796875 to 1.796875
- param_offsets: int32 [2, 128, 4], replicated, may hold values from 0 to 622336, as said below
- owner_map: int32 [2, 128], replicated, may hold values from 0 to 31, as said below
- slice_map: int32 [32, 8], replicated, may hold values from 0 to 7, each once within a row
Outputs:
- query_absorbed: bfloat16 [2, 128, 1536, 512], P(None, 'fsdp', 'tp')
- output_absorbed: bfloat16 [2, 128, 7168, 512], P(None, 'fsdp', 'tp')
Inputs may be any that keep to these rules, and one draw needn't show every extreme that they name: `param_offsets`: in each layer the pieces of all heads' four parameters lie in a rank's 622592 entries one after another in some order, without gaps or intersections; a piece of a parameter holds that parameter's entries divided by 256; the last piece of each layer is a key up-projection piece. `owner_map`: in each layer every index of fsdp owns exactly 4 heads.
All inputs are finite; a program needn't handle non-finite values.
Results may differ from a plain program's by a relative error of at most 0.001.
Values may be sent and summed in bfloat16 or wider, within the bound.
A program may use at most 64 MiB of HBM per device.

v0:
```python
import math
import jax
import jax.numpy as jnp
from jax import lax
from jax.sharding import PartitionSpec as P

D = 7168
QR = 1536
KVR = 512
QK_NOPE = 128
V_DIM = 128


def for_sending(shard):
    return jax.tree.map(lambda a: a.astype(jnp.bfloat16) if a.dtype == jnp.float32 else a, shard)


def head_order(owner_map, per_group):
    head_count = owner_map.shape[1]
    head_index = jnp.arange(head_count, dtype=jnp.int32)
    same_owner = owner_map[:, :, None] == owner_map[:, None, :]
    before = head_index[None, None, :] < head_index[None, :, None]
    head_rank = jnp.sum(jnp.logical_and(same_owner, before).astype(jnp.int32), axis=2)
    head_slot = owner_map * per_group + head_rank
    slot_hits = head_slot[:, :, None] == head_index[None, None, :]
    return jnp.sum(jnp.where(slot_hits, head_index[None, :, None], 0), axis=1)


def cut_pieces(local_flat, begins, width_now, granule):
    layer_count, heads_here = begins.shape
    row_table = local_flat.reshape(layer_count, local_flat.shape[1] // granule, granule)
    row_steps = jnp.arange(width_now // granule, dtype=jnp.int32)
    row_ids = (begins[:, :, None] // granule + row_steps[None, None, :]).reshape(
        layer_count, heads_here * (width_now // granule)
    )
    picked = jnp.take_along_axis(row_table, row_ids[:, :, None], axis=1)
    return picked.reshape(layer_count, heads_here, width_now)


def refresh(local_flat, param_offsets, head_at, slice_row):
    fsdp_ways = lax.axis_size("fsdp")
    tensor_ways = lax.axis_size("tp")
    rank_total = fsdp_ways * tensor_ways
    layer_count = local_flat.shape[0]
    per_group = head_at.shape[1] // fsdp_ways
    widths = (
        QR * QK_NOPE // rank_total,
        QK_NOPE * KVR // rank_total,
        V_DIM * KVR // rank_total,
        D * V_DIM // rank_total,
    )
    granule = math.gcd(math.gcd(widths[0], widths[1]), math.gcd(widths[2], widths[3]))
    begins = jnp.take_along_axis(param_offsets, head_at[:, :, None], axis=1)
    pieces = tuple(
        (
            cut_pieces(local_flat, begins[:, :, kind_id], widths[kind_id], granule).reshape(
                layer_count, fsdp_ways, per_group, 1, widths[kind_id]
            )
            for kind_id in range(4)
        )
    )
    arrived = jax.tree.map(
        lambda part, own: part.astype(own.dtype),
        lax.all_to_all(for_sending(pieces), "fsdp", split_axis=1, concat_axis=3, tiled=True),
        pieces,
    )
    query_part, key_part, value_part, out_part = tuple(
        (
            arrived[kind_id].reshape(layer_count, per_group, fsdp_ways, 1, widths[kind_id])
            for kind_id in range(4)
        )
    )
    slice_query = QR // tensor_ways
    slice_output = D // tensor_ways
    blocks = fsdp_ways // tensor_ways

    def to_send(part_in, width_now):
        grouped = part_in.reshape(layer_count, per_group, tensor_ways, blocks, width_now)
        return jnp.take(grouped, slice_row, axis=2).reshape(
            layer_count, per_group, tensor_ways, blocks, 1, width_now
        )

    query_rows, out_rows = (
        lax.all_to_all(
            to_send(query_part, widths[0]), "tp", split_axis=2, concat_axis=4, tiled=True
        ),
        lax.all_to_all(to_send(out_part, widths[3]), "tp", split_axis=2, concat_axis=4, tiled=True),
    )
    query_rows = query_rows.reshape(layer_count, per_group, slice_query, QK_NOPE)
    out_rows = out_rows.reshape(layer_count, per_group, slice_output, V_DIM)
    key_full, value_full = (
        lax.all_gather(key_part, "tp", axis=3, tiled=True),
        lax.all_gather(value_part, "tp", axis=3, tiled=True),
    )
    key_full = key_full.reshape(layer_count, per_group, QK_NOPE, KVR)
    value_full = value_full.reshape(layer_count, per_group, V_DIM, KVR)
    query_absorbed = jnp.einsum(
        "lhrc,lhck->lhrk", query_rows, key_full, preferred_element_type=jnp.float32
    ).astype(jnp.bfloat16)
    output_absorbed = jnp.einsum(
        "lhrc,lhck->lhrk", out_rows, value_full, preferred_element_type=jnp.float32
    ).astype(jnp.bfloat16)
    return (query_absorbed, output_absorbed)


def per_device(learner_flat, param_offsets, owner_map, slice_map):
    fsdp_ways = lax.axis_size("fsdp")
    per_group = owner_map.shape[1] // fsdp_ways
    head_at = head_order(owner_map, per_group)
    slice_row = lax.dynamic_index_in_dim(slice_map, lax.axis_index("fsdp"), 0, keepdims=False)
    layer_results = [
        refresh(
            learner_flat[layer_id : layer_id + 1],
            param_offsets[layer_id : layer_id + 1],
            head_at[layer_id : layer_id + 1],
            slice_row,
        )
        for layer_id in range(learner_flat.shape[0])
    ]
    query_absorbed = jnp.concatenate([result_pair[0] for result_pair in layer_results], axis=0)
    output_absorbed = jnp.concatenate([result_pair[1] for result_pair in layer_results], axis=0)
    return (query_absorbed, output_absorbed)


def solution(mesh):
    placed = (P(None, ("fsdp", "tp")), P(), P(), P())
    return jax.shard_map(
        per_device,
        mesh=mesh,
        in_specs=placed,
        out_specs=(P(None, "fsdp", "tp", None), P(None, "fsdp", "tp", None)),
        check_vma=False,
    )
```

profile of v0, /device:TPU:38, one launch (start us, length us, event | category | flops | bytes accessed | tf_op | source)
XLA Modules:
  0.0 371.7 jit_solution(2697430013469942218)
XLA Ops:
  4.4 28.8 %slice_reduce_fusion.1 = (bf16[622592]{0:T(1024)(128)(2,1)S(1)}, bf16[622592]{0:T(1024)(128)(2,1)}) fusion(bf16[2,622592]{1,0:T(2,128)(2,1)} %param.16), kind=kLoop, calls=%fused_computation.18 | loop fusion | bytes 4980736 | tf_op jit(solution)/shard_map/slice | solution.py:113
  35.2 7.6 %all-to-all-start.8 = ((bf16[1,32,4,1,256]{4,2,3,0,1:T(4,128)(2,1)}), bf16[1,32,4,1,256]{4,2,3,0,1:T(4,128)(2,1)S(1)}, u32[]{:S(2)}, u32[]{:S(2)}) async-start(bf16[1,32,4,1,256]{4,2,3,0,1:T(4,128)(2,1)} %bitcast.57), calls=%async_computation.8 | async-start | bytes 131072 | tf_op jit(solution)/shard_map/all_to_all | solution.py:64
  46.9 2.1 gather_fusion.1
  48.9 2.2 reshape.662
  55.8 7.4 %all-to-all-start.2 = ((bf16[1,32,4,1,256]{4,2,3,0,1:T(4,128)(2,1)}), bf16[1,32,4,1,256]{4,2,3,0,1:T(4,128)(2,1)S(1)}, u32[]{:S(2)}, u32[]{:S(2)}) async-start(bf16[1,32,4,1,256]{4,2,3,0,1:T(4,128)(2,1)} %bitcast.18), calls=%async_computation.2 | async-start | bytes 131072 | tf_op jit(solution)/shard_map/all_to_all | solution.py:64
  63.2 1.2 and_reduce_fusion.5
  65.1 3.8 %all-to-all-done.2 = bf16[1,32,4,1,256]{4,2,3,0,1:T(4,128)(2,1)S(1)} async-done(((bf16[1,32,4,1,256]{4,2,3,0,1:T(4,128)(2,1)}), bf16[1,32,4,1,256]{4,2,3,0,1:T(4,128)(2,1)S(1)}, u32[]{:S(2)}, u32[]{:S(2)}) %all-to-all-start.2) | async-done | bytes 65568 | tf_op jit(solution)/shard_map/all_to_all | solution.py:64
  68.9 6.2 %all-to-all-start.11 = ((bf16[1,32,4,1,256]{4,2,3,0,1:T(4,128)(2,1)}), bf16[1,32,4,1,256]{4,2,3,0,1:T(4,128)(2,1)}, u32[]{:S(2)}, u32[]{:S(2)}) async-start(bf16[1,32,4,1,256]{4,2,3,0,1:T(4,128)(2,1)} %bitcast.74), calls=%async_computation.11 | async-start | bytes 131072 | tf_op jit(solution)/shard_map/all_to_all | solution.py:64
  75.1 5.5 %gather_fusion.8 = bf16[1792,256]{1,0:T(8,128)(2,1)S(1)} fusion(bf16[2432,256]{1,0:T(8,128)(2,1)S(1)} %reshape.643, s32[2048]{0:T(1024)S(1)} %pad_clamp_fusion.1), kind=kCustom, calls=%fused_computation.4.clone | custom fusion | bytes 1842176 | tf_op jit(solution)/shard_map/jit(take_along_axis)/gather | solution.py:36
  80.6 1.7 reshape_reshape.24
  82.3 1.5 reshape.457
  83.8 7.5 %all-to-all-start.5 = ((bf16[1,32,4,1,256]{4,2,3,0,1:T(4,128)(2,1)}), bf16[1,32,4,1,256]{4,2,3,0,1:T(4,128)(2,1)S(1)}, u32[]{:S(2)}, u32[]{:S(2)}) async-start(bf16[1,32,4,1,256]{4,2,3,0,1:T(4,128)(2,1)} %bitcast.40), calls=%async_computation.5 | async-start | bytes 131072 | tf_op jit(solution)/shard_map/all_to_all | solution.py:64
  91.3 2.1 gather_fusion.5
  93.4 3.6 all-to-all-done.5
  97.6 5.6 %all-to-all-start = ((bf16[1,32,4,1,768]{4,2,3,0,1:T(4,128)(2,1)}), bf16[1,32,4,1,768]{4,2,3,0,1:T(4,128)(2,1)S(1)}, u32[]{:S(2)}, u32[]{:S(2)}) async-start(bf16[1,32,4,1,768]{4,2,3,0,1:T(4,128)(2,1)} %bitcast.6), calls=%async_computation | async-start | bytes 393216 | tf_op jit(solution)/shard_map/all_to_all | solution.py:64
  104.1 5.7 %all-to-all-done = bf16[1,32,4,1,768]{4,2,3,0,1:T(4,128)(2,1)S(1)} async-done(((bf16[1,32,4,1,768]{4,2,3,0,1:T(4,128)(2,1)}), bf16[1,32,4,1,768]{4,2,3,0,1:T(4,128)(2,1)S(1)}, u32[]{:S(2)}, u32[]{:S(2)}) %all-to-all-start) | async-done | bytes 196640 | tf_op jit(solution)/shard_map/all_to_all | solution.py:64
  109.8 5.5 %all-to-all-start.3 = ((bf16[1,32,4,1,768]{4,2,3,0,1:T(4,128)(2,1)}), bf16[1,32,4,1,768]{4,2,3,0,1:T(4,128)(2,1)S(1)}, u32[]{:S(2)}, u32[]{:S(2)}) async-start(bf16[1,32,4,1,768]{4,2,3,0,1:T(4,128)(2,1)} %bitcast.28), calls=%async_computation.3 | async-start | bytes 393216 | tf_op jit(solution)/shard_map/all_to_all | solution.py:64
  115.6 1.3 reshape_reshape.28
  116.9 4.9 %all-to-all-done.3 = bf16[1,32,4,1,768]{4,2,3,0,1:T(4,128)(2,1)S(1)} async-done(((bf16[1,32,4,1,768]{4,2,3,0,1:T(4,128)(2,1)}), bf16[1,32,4,1,768]{4,2,3,0,1:T(4,128)(2,1)S(1)}, u32[]{:S(2)}, u32[]{:S(2)}) %all-to-all-start.3) | async-done | bytes 196640 | tf_op jit(solution)/shard_map/all_to_all | solution.py:64
  121.9 5.5 %all-to-all-start.6 = ((bf16[1,32,4,1,3584]{4,2,3,0,1:T(4,128)(2,1)}), bf16[1,32,4,1,3584]{4,2,3,0,1:T(4,128)(2,1)S(1)}, u32[]{:S(2)}, u32[]{:S(2)}) async-start(bf16[1,32,4,1,3584]{4,2,3,0,1:T(4,128)(2,1)} %bitcast.45), calls=%async_computation.6 | async-start | bytes 1835008 | tf_op jit(solution)/shard_map/all_to_all | solution.py:64
  127.4 5.5 %gather_fusion.11 = bf16[1792,256]{1,0:T(8,128)(2,1)S(1)} fusion(bf16[2432,256]{1,0:T(8,128)(2,1)S(1)} %reshape.662, s32[2048]{0:T(1024)S(1)} %pad_clamp_fusion), kind=kCustom, calls=%fused_computation.12.clone | custom fusion | bytes 1842176 | tf_op jit(solution)/shard_map/jit(take_along_axis)/gather | solution.py:36
  133.2 1.3 reshape_reshape.30
  134.5 6.2 %all-to-all-done.6 = bf16[1,32,4,1,3584]{4,2,3,0,1:T(4,128)(2,1)S(1)} async-done(((bf16[1,32,4,1,3584]{4,2,3,0,1:T(4,128)(2,1)}), bf16[1,32,4,1,3584]{4,2,3,0,1:T(4,128)(2,1)S(1)}, u32[]{:S(2)}, u32[]{:S(2)}) %all-to-all-start.6) | async-done | bytes 917536 | tf_op jit(solution)/shard_map/all_to_all | solution.py:64
  140.7 6.4 %all-to-all-start.9 = ((bf16[1,32,4,1,3584]{4,2,3,0,1:T(4,128)(2,1)}), bf16[1,32,4,1,3584]{4,2,3,0,1:T(4,128)(2,1)S(1)}, u32[]{:S(2)}, u32[]{:S(2)}) async-start(bf16[1,32,4,1,3584]{4,2,3,0,1:T(4,128)(2,1)} %bitcast.62), calls=%async_computation.9 | async-start | bytes 1835008 | tf_op jit(solution)/shard_map/all_to_all | solution.py:64
  149.9 10.5 %all-to-all-done.9 = bf16[1,32,4,1,3584]{4,2,3,0,1:T(4,128)(2,1)S(1)} async-done(((bf16[1,32,4,1,3584]{4,2,3,0,1:T(4,128)(2,1)}), bf16[1,32,4,1,3584]{4,2,3,0,1:T(4,128)(2,1)S(1)}, u32[]{:S(2)}, u32[]{:S(2)}) %all-to-all-start.9) | async-done | bytes 917536 | tf_op jit(solution)/shard_map/all_to_all | solution.py:64
  160.4 8.6 %all-to-all-start.1 = ((bf16[1,4,8,4,1,768]{5,3,1,4,0,2:T(4,128)(2,1)}), bf16[1,4,8,4,1,768]{5,3,1,4,0,2:T(4,128)(2,1)S(1)}, u32[]{:S(2)}, u32[]{:S(2)}) async-start(bf16[1,4,8,4,1,768]{5,3,1,4,0,2:T(4,128)(2,1)} %get-tuple-element.46), calls=%async_computation.1 | async-start | bytes 393216 | tf_op jit(solution)/shard_map/all_to_all | solution.py:84
  169.4 1.3 gather_fusion.9
  171.1 1.3 gather_fusion.12
  172.4 7.0 %all-to-all-done.1 = bf16[1,4,8,4,1,768]{5,3,1,4,0,2:T(4,128)(2,1)S(1)} async-done(((bf16[1,4,8,4,1,768]{5,3,1,4,0,2:T(4,128)(2,1)}), bf16[1,4,8,4,1,768]{5,3,1,4,0,2:T(4,128)(2,1)S(1)}, u32[]{:S(2)}, u32[]{:S(2)}) %all-to-all-start.1) | async-done | bytes 196640 | tf_op jit(solution)/shard_map/all_to_all | solution.py:84
  179.4 4.8 %all-to-all-start.4 = ((bf16[1,4,8,4,1,768]{5,3,1,4,0,2:T(4,128)(2,1)}), bf16[1,4,8,4,1,768]{5,3,1,4,0,2:T(4,128)(2,1)S(1)}, u32[]{:S(2)}, u32[]{:S(2)}) async-start(bf16[1,4,8,4,1,768]{5,3,1,4,0,2:T(4,128)(2,1)} %get-tuple-element.47), calls=%async_computation.4 | async-start | bytes 393216 | tf_op jit(solution)/shard_map/all_to_all | solution.py:84
  184.2 1.8 fusion.3
  186.0 7.8 %all-to-all-done.4 = bf16[1,4,8,4,1,768]{5,3,1,4,0,2:T(4,128)(2,1)S(1)} async-done(((bf16[1,4,8,4,1,768]{5,3,1,4,0,2:T(4,128)(2,1)}), bf16[1,4,8,4,1,768]{5,3,1,4,0,2:T(4,128)(2,1)S(1)}, u32[]{:S(2)}, u32[]{:S(2)}) %all-to-all-start.4) | async-done | bytes 196640 | tf_op jit(solution)/shard_map/all_to_all | solution.py:84
  193.8 27.8 %all_to_all.180 = bf16[1,4,8,4,1,3584]{5,3,1,4,0,2:T(4,128)(2,1)S(1)} all-to-all(bf16[1,4,8,4,1,3584]{5,3,1,4,0,2:T(4,128)(2,1)S(1)} %get-tuple-element.44), channel_id=1, replica_groups=mesh['fsdp'=32,'tp'=8] {'tp'}, dimensions={2} | all-to-all | bytes 1835008 | tf_op jit(solution)/shard_map/all_to_all | solution.py:87
  221.6 4.9 %all-to-all-start.10 = ((bf16[1,4,8,4,1,3584]{5,3,1,4,0,2:T(4,128)(2,1)}), bf16[1,4,8,4,1,3584]{5,3,1,4,0,2:T(4,128)(2,1)S(1)}, u32[]{:S(2)}, u32[]{:S(2)}) async-start(bf16[1,4,8,4,1,3584]{5,3,1,4,0,2:T(4,128)(2,1)} %get-tuple-element.45), calls=%async_computation.10 | async-start | bytes 1835008 | tf_op jit(solution)/shard_map/all_to_all | solution.py:87
  226.5 41.6 %all-gather = bf16[1,1,4,32,8,256]{5,3,4,2,1,0:T(8,128)(2,1)S(1)} all-gather(bf16[1,1,4,32,1,256]{5,3,4,2,1,0:T(8,128)(2,1)S(1)} %bitcast.216), channel_id=2, replica_groups=mesh['fsdp'=32,'tp'=8] {'tp'}, dimensions={4}, use_global_device_ids=true | all-gather | bytes 589824 | tf_op jit(solution)/shard_map/all_gather | solution.py:92
  268.6 25.5 %all-gather.2 = bf16[1,1,4,32,8,256]{5,3,4,2,1,0:T(8,128)(2,1)S(1)} all-gather(bf16[1,1,4,32,1,256]{5,3,4,2,1,0:T(8,128)(2,1)S(1)} %bitcast.217), channel_id=4, replica_groups=mesh['fsdp'=32,'tp'=8] {'tp'}, dimensions={4}, use_global_device_ids=true | all-gather | bytes 589824 | tf_op jit(solution)/shard_map/all_gather | solution.py:93
  294.6 25.5 %all-gather.1 = bf16[1,1,4,32,8,256]{5,3,4,2,1,0:T(8,128)(2,1)S(1)} all-gather(bf16[1,1,4,32,1,256]{5,3,4,2,1,0:T(8,128)(2,1)S(1)} %bitcast.218), channel_id=3, replica_groups=mesh['fsdp'=32,'tp'=8] {'tp'}, dimensions={4}, use_global_device_ids=true | all-gather | bytes 589824 | tf_op jit(solution)/shard_map/all_gather | solution.py:92
  321.2 1.2 reshape.459
  323.3 25.2 %all-gather.3 = bf16[1,1,4,32,8,256]{5,3,4,2,1,0:T(8,128)(2,1)S(1)} all-gather(bf16[1,1,4,32,1,256]{5,3,4,2,1,0:T(8,128)(2,1)S(1)} %bitcast.219), channel_id=5, replica_groups=mesh['fsdp'=32,'tp'=8] {'tp'}, dimensions={4}, use_global_device_ids=true | all-gather | bytes 589824 | tf_op jit(solution)/shard_map/all_gather | solution.py:93
  349.6 2.0 reshape.469
  351.6 1.7 copy.94
  353.3 1.8 reshape.450
  355.0 1.7 copy.102
  356.7 1.8 reshape.456
  358.5 1.3 fusion
  360.2 1.3 pad_maximum_fusion.1
  364.8 2.1 convert_bitcast_fusion
  368.1 3.7 pad_maximum_fusion
  (122 shorter events, 29.5 us)
Async XLA Ops:
  0.6 146.5 %copy-start = (s32[32,8]{0,1:T(8,128)S(1)}, s32[32,8]{0,1:T(8,128)}, u32[]{:S(2)}) copy-start(s32[32,8]{0,1:T(8,128)} %param.19) | copy-start | bytes 3076
  35.2 20.7 %all-to-all-start.8 = ((bf16[1,32,4,1,256]{4,2,3,0,1:T(4,128)(2,1)}), bf16[1,32,4,1,256]{4,2,3,0,1:T(4,128)(2,1)S(1)}, u32[]{:S(2)}, u32[]{:S(2)}) async-start(bf16[1,32,4,1,256]{4,2,3,0,1:T(4,128)(2,1)} %bitcast.57), calls=%async_computation.8 | async-start | bytes 131072 | tf_op jit(solution)/shard_map/all_to_all | solution.py:64
  55.8 13.1 %all-to-all-start.2 = ((bf16[1,32,4,1,256]{4,2,3,0,1:T(4,128)(2,1)}), bf16[1,32,4,1,256]{4,2,3,0,1:T(4,128)(2,1)S(1)}, u32[]{:S(2)}, u32[]{:S(2)}) async-start(bf16[1,32,4,1,256]{4,2,3,0,1:T(4,128)(2,1)} %bitcast.18), calls=%async_computation.2 | async-start | bytes 131072 | tf_op jit(solution)/shard_map/all_to_all | solution.py:64
  68.9 14.9 %all-to-all-start.11 = ((bf16[1,32,4,1,256]{4,2,3,0,1:T(4,128)(2,1)}), bf16[1,32,4,1,256]{4,2,3,0,1:T(4,128)(2,1)}, u32[]{:S(2)}, u32[]{:S(2)}) async-start(bf16[1,32,4,1,256]{4,2,3,0,1:T(4,128)(2,1)} %bitcast.74), calls=%async_computation.11 | async-start | bytes 131072 | tf_op jit(solution)/shard_map/all_to_all | solution.py:64
  80.6 22.6 %copy-start.13 = (pred[384]{0:T(512)(128)(4,1)S(1)}, pred[384]{0:T(512)(128)(4,1)}, u32[]{:S(2)}) copy-start(pred[384]{0:T(512)(128)(4,1)} %get-tuple-element.38) | copy-start | bytes 1156
  83.8 13.2 %all-to-all-start.5 = ((bf16[1,32,4,1,256]{4,2,3,0,1:T(4,128)(2,1)}), bf16[1,32,4,1,256]{4,2,3,0,1:T(4,128)(2,1)S(1)}, u32[]{:S(2)}, u32[]{:S(2)}) async-start(bf16[1,32,4,1,256]{4,2,3,0,1:T(4,128)(2,1)} %bitcast.40), calls=%async_computation.5 | async-start | bytes 131072 | tf_op jit(solution)/shard_map/all_to_all | solution.py:64
  91.3 24.0 %copy-start.12 = (pred[1792]{0:T(1024)(128)(4,1)S(1)}, pred[1792]{0:T(1024)(128)(4,1)}, u32[]{:S(2)}) copy-start(pred[1792]{0:T(1024)(128)(4,1)} %get-tuple-element.16) | copy-start | bytes 5380
  97.0 0.6 copy-start.8
  97.6 12.2 %all-to-all-start = ((bf16[1,32,4,1,768]{4,2,3,0,1:T(4,128)(2,1)}), bf16[1,32,4,1,768]{4,2,3,0,1:T(4,128)(2,1)S(1)}, u32[]{:S(2)}, u32[]{:S(2)}) async-start(bf16[1,32,4,1,768]{4,2,3,0,1:T(4,128)(2,1)} %bitcast.6), calls=%async_computation | async-start | bytes 393216 | tf_op jit(solution)/shard_map/all_to_all | solution.py:64
  109.8 5.5 %copy-start.1 = (bf16[1,32,4,1,768]{4,2,3,0,1:T(4,128)(2,1)}, bf16[1,32,4,1,768]{4,2,3,0,1:T(4,128)(2,1)S(1)}, u32[]{:S(2)}) copy-start(bf16[1,32,4,1,768]{4,2,3,0,1:T(4,128)(2,1)S(1)} %all-to-all-done) | copy-start | bytes 589828
  109.8 12.1 %all-to-all-start.3 = ((bf16[1,32,4,1,768]{4,2,3,0,1:T(4,128)(2,1)}), bf16[1,32,4,1,768]{4,2,3,0,1:T(4,128)(2,1)S(1)}, u32[]{:S(2)}, u32[]{:S(2)}) async-start(bf16[1,32,4,1,768]{4,2,3,0,1:T(4,128)(2,1)} %bitcast.28), calls=%async_computation.3 | async-start | bytes 393216 | tf_op jit(solution)/shard_map/all_to_all | solution.py:64
  115.6 11.7 %copy-start.10 = (s32[1,1792,1]{1,2,0:T(1,128)S(1)}, s32[1,1792,1]{1,2,0:T(1,128)}, u32[]{:S(2)}) copy-start(s32[1,1792,1]{1,2,0:T(1,128)} %get-tuple-element.35) | copy-start | bytes 21508
  121.9 11.0 %copy-start.4 = (bf16[1,32,4,1,768]{4,2,3,0,1:T(4,128)(2,1)}, bf16[1,32,4,1,768]{4,2,3,0,1:T(4,128)(2,1)S(1)}, u32[]{:S(2)}) copy-start(bf16[1,32,4,1,768]{4,2,3,0,1:T(4,128)(2,1)S(1)} %all-to-all-done.3) | copy-start | bytes 589828
  121.9 18.8 %all-to-all-start.6 = ((bf16[1,32,4,1,3584]{4,2,3,0,1:T(4,128)(2,1)}), bf16[1,32,4,1,3584]{4,2,3,0,1:T(4,128)(2,1)S(1)}, u32[]{:S(2)}, u32[]{:S(2)}) async-start(bf16[1,32,4,1,3584]{4,2,3,0,1:T(4,128)(2,1)} %bitcast.45), calls=%async_computation.6 | async-start | bytes 1835008 | tf_op jit(solution)/shard_map/all_to_all | solution.py:64
  127.4 5.5 %copy-start.11 = (pred[1792]{0:T(1024)(128)(4,1)S(1)}, pred[1792]{0:T(1024)(128)(4,1)}, u32[]{:S(2)}) copy-start(pred[1792]{0:T(1024)(128)(4,1)} %get-tuple-element.34) | copy-start | bytes 5380
  133.2 14.1 %copy-start.2 = (bf16[1,32,4,1,768]{4,2,3,0,1:T(4,128)(2,1)S(1)}, bf16[1,32,4,1,768]{4,2,3,0,1:T(4,128)(2,1)}, u32[]{:S(2)}) copy-start(bf16[1,32,4,1,768]{4,2,3,0,1:T(4,128)(2,1)} %copy-done.1) | copy-start | bytes 589828
  134.5 12.9 %copy-start.5 = (bf16[1,32,4,1,768]{4,2,3,0,1:T(4,128)(2,1)S(1)}, bf16[1,32,4,1,768]{4,2,3,0,1:T(4,128)(2,1)}, u32[]{:S(2)}) copy-start(bf16[1,32,4,1,768]{4,2,3,0,1:T(4,128)(2,1)} %copy-done.4) | copy-start | bytes 589828
  140.7 19.8 %all-to-all-start.9 = ((bf16[1,32,4,1,3584]{4,2,3,0,1:T(4,128)(2,1)}), bf16[1,32,4,1,3584]{4,2,3,0,1:T(4,128)(2,1)S(1)}, u32[]{:S(2)}, u32[]{:S(2)}) async-start(bf16[1,32,4,1,3584]{4,2,3,0,1:T(4,128)(2,1)} %bitcast.62), calls=%async_computation.9 | async-start | bytes 1835008 | tf_op jit(solution)/shard_map/all_to_all | solution.py:64
  160.4 19.0 %all-to-all-start.1 = ((bf16[1,4,8,4,1,768]{5,3,1,4,0,2:T(4,128)(2,1)}), bf16[1,4,8,4,1,768]{5,3,1,4,0,2:T(4,128)(2,1)S(1)}, u32[]{:S(2)}, u32[]{:S(2)}) async-start(bf16[1,4,8,4,1,768]{5,3,1,4,0,2:T(4,128)(2,1)} %get-tuple-element.46), calls=%async_computation.1 | async-start | bytes 393216 | tf_op jit(solution)/shard_map/all_to_all | solution.py:84
  179.4 6.6 %copy-start.3 = (bf16[1,4,8,4,1,768]{5,3,1,4,0,2:T(4,128)(2,1)}, bf16[1,4,8,4,1,768]{5,3,1,4,0,2:T(4,128)(2,1)S(1)}, u32[]{:S(2)}) copy-start(bf16[1,4,8,4,1,768]{5,3,1,4,0,2:T(4,128)(2,1)S(1)} %all-to-all-done.1) | copy-start | bytes 589828
  179.4 14.4 %all-to-all-start.4 = ((bf16[1,4,8,4,1,768]{5,3,1,4,0,2:T(4,128)(2,1)}), bf16[1,4,8,4,1,768]{5,3,1,4,0,2:T(4,128)(2,1)S(1)}, u32[]{:S(2)}, u32[]{:S(2)}) async-start(bf16[1,4,8,4,1,768]{5,3,1,4,0,2:T(4,128)(2,1)} %get-tuple-element.47), calls=%async_computation.4 | async-start | bytes 393216 | tf_op jit(solution)/shard_map/all_to_all | solution.py:84
  193.8 27.8 %copy-start.6 = (bf16[1,4,8,4,1,768]{5,3,1,4,0,2:T(4,128)(2,1)}, bf16[1,4,8,4,1,768]{5,3,1,4,0,2:T(4,128)(2,1)S(1)}, u32[]{:S(2)}) copy-start(bf16[1,4,8,4,1,768]{5,3,1,4,0,2:T(4,128)(2,1)S(1)} %all-to-all-done.4) | copy-start | bytes 589828
  221.6 141.6 %all-to-all-start.10 = ((bf16[1,4,8,4,1,3584]{5,3,1,4,0,2:T(4,128)(2,1)}), bf16[1,4,8,4,1,3584]{5,3,1,4,0,2:T(4,128)(2,1)S(1)}, u32[]{:S(2)}, u32[]{:S(2)}) async-start(bf16[1,4,8,4,1,3584]{5,3,1,4,0,2:T(4,128)(2,1)} %get-tuple-element.45), calls=%async_computation.10 | async-start | bytes 1835008 | tf_op jit(solution)/shard_map/all_to_all | solution.py:87
  268.6 26.0 %copy-start.9 = (bf16[1,32,4,1,256]{4,2,3,0,1:T(4,128)(2,1)S(1)}, bf16[1,32,4,1,256]{4,2,3,0,1:T(4,128)(2,1)}, u32[]{:S(2)}) copy-start(bf16[1,32,4,1,256]{4,2,3,0,1:T(4,128)(2,1)} %copy-done.8) | copy-start | bytes 196612
  358.5 1.3 copy-start.7
where the time goes:
time: 373 us; the launch traced here: 372 us
  blocking collectives  146 us (39%)
  local copies, waits for them, and re-layouts  85.3 us (23%)
  starting transfers between devices  69.7 us (19%)
  waiting for transfers between devices  49.5 us (13%)
  other arithmetic  15.4 us (4%)
  matrix products  4.9 us (1%)
    all_gather x2, blocking collectives, refresh(): lax.all_gather(key_part, 'tp', axis=3, tiled=True)  67.1 us
    all_to_all x8, starting transfers between devices, refresh(): lax.all_to_all(for_sending(pieces), 'fsdp', split_axis=1, concat_axis=3,...  51.5 us
    all_gather x2, blocking collectives, refresh(): lax.all_gather(value_part, 'tp', axis=3, tiled=True)  50.7 us
    all_to_all x8, waiting for transfers between devices, refresh(): lax.all_to_all(for_sending(pieces), 'fsdp', split_axis=1, concat_axis=3,...  34.7 us
    slice x1, local copies, waits for them, and re-layouts, per_device(): learner_flat[layer_id:layer_id + 1]  28.8 us
    all_to_all x1, blocking collectives, refresh(): lax.all_to_all(to_send(out_part, widths[3]), 'tp', split_axis=2, concat_a...  27.8 us
    gather x8, local copies, waits for them, and re-layouts, cut_pieces(): picked = jnp.take_along_axis(row_table, row_ids[:, :, None], axis=1)  18.4 us
    all_to_all x2, waiting for transfers between devices, refresh(): lax.all_to_all(to_send(query_part, widths[0]), 'tp', split_axis=2, concat...  14.8 us
  transfers between devices with their start and end apart: 11, of which 8 were waited for; matrix products, arithmetic and copies ran while one was open for 17% of the time, Pallas kernels for 0%

commit v1 on v0

--- a/solution.py
+++ b/solution.py
@@ -90,7 +90,9 @@
     out_rows = out_rows.reshape(layer_count, per_group, slice_output, V_DIM)
     key_full, value_full = (
         lax.all_gather(key_part, "tp", axis=3, tiled=True),
-        lax.all_gather(value_part, "tp", axis=3, tiled=True),
+        jnp.concatenate(
+            lax.all_to_all(jnp.stack([value_part] * lax.axis_size("tp")), "tp", 0, 0), axis=3
+        ),
     )
     key_full = key_full.reshape(layer_count, per_group, QK_NOPE, KVR)
     value_full = value_full.reshape(layer_count, per_group, V_DIM, KVR)

time: 373 us -> 361 us (0.968)
  blocking collectives: 146 us -> 97 us
  waiting for transfers between devices: 49.5 us -> 81.4 us
  starting transfers between devices: 69.7 us -> 79.1 us
  local copies, waits for them, and re-layouts: 85.3 us -> 80 us
    all_gather x2 -> x0, blocking collectives: 50.7 us -> none  [refresh(): lax.all_gather(value_part, 'tp', axis=3, tiled=True)]
    all_to_all x0 -> x2, waiting for transfers between devices: none -> 28.8 us  [refresh(): lax.all_to_all(jnp.stack([value_part] * lax.axis_size('tp')), 'tp', 0, 0)]
    all_to_all x0 -> x2, starting transfers between devices: none -> 11.2 us  [refresh(): lax.all_to_all(jnp.stack([value_part] * lax.axis_size('tp')), 'tp', 0, 0)]
    all_to_all x8, waiting for transfers between devices: 34.7 us -> 44.2 us  [refresh(): lax.all_to_all(for_sending(pieces), 'fsdp', split_axis=1, concat_axis=3,...]
    all_to_all x2, waiting for transfers between devices: 14.8 us -> 8.47 us  [refresh(): lax.all_to_all(to_send(query_part, widths[0]), 'tp', split_axis=2, concat...]
    another operation x8 -> x12, local copies, waits for them, and re-layouts: 9.43 us -> 8.41 us
  transfers between devices with their start and end apart: 11 -> 13, of which waited for: 8 -> 11; matrix products, arithmetic and copies ran while one was open for 17% -> 15% of each run, Pallas kernels for 0% -> 0%
where the time goes in v1:
time: 361 us; the launch traced here: 358 us
  blocking collectives  97 us (27%)
  waiting for transfers between devices  81.4 us (23%)
  local copies, waits for them, and re-layouts  80 us (22%)
  starting transfers between devices  79.1 us (22%)
  other arithmetic  14.3 us (4%)
  matrix products  4.92 us (1%)
    all_gather x2, blocking collectives, refresh(): lax.all_gather(key_part, 'tp', axis=3, tiled=True)  68 us
    all_to_all x8, starting transfers between devices, refresh(): lax.all_to_all(for_sending(pieces), 'fsdp', split_axis=1, concat_axis=3,...  49.2 us
    all_to_all x8, waiting for transfers between devices, refresh(): lax.all_to_all(for_sending(pieces), 'fsdp', split_axis=1, concat_axis=3,...  44.2 us
    all_to_all x1, blocking collectives, refresh(): lax.all_to_all(to_send(out_part, widths[3]), 'tp', split_axis=2, concat_a...  29 us
    slice x1, local copies, waits for them, and re-layouts, per_device(): learner_flat[layer_id:layer_id + 1]  28.8 us
    all_to_all x2, waiting for transfers between devices, refresh(): lax.all_to_all(jnp.stack([value_part] * lax.axis_size('tp')), 'tp', 0, 0)  28.8 us
    gather x8, local copies, waits for them, and re-layouts, cut_pieces(): picked = jnp.take_along_axis(row_table, row_ids[:, :, None], axis=1)  18.4 us
    all_to_all x2, starting transfers between devices, refresh(): lax.all_to_all(to_send(query_part, widths[0]), 'tp', split_axis=2, concat...  13.8 us
  transfers between devices with their start and end apart: 13, of which 11 were waited for; matrix products, arithmetic and copies ran while one was open for 15% of the time, Pallas kernels for 0%

profile of v1, /device:TPU:38, one launch (start us, length us, event | category | flops | bytes accessed | tf_op | source)
XLA Modules:
  0.0 358.0 jit_solution(1798388790356269182)
XLA Ops:
  4.4 28.8 %slice_reduce_fusion.1 = (bf16[622592]{0:T(1024)(128)(2,1)S(1)}, bf16[622592]{0:T(1024)(128)(2,1)}) fusion(bf16[2,622592]{1,0:T(2,128)(2,1)} %param.16), kind=kLoop, calls=%fused_computation.18 | loop fusion | bytes 4980736 | tf_op jit(solution)/shard_map/slice | solution.py:115
  35.2 7.6 %all-to-all-start.8 = ((bf16[1,32,4,1,256]{4,2,3,0,1:T(4,128)(2,1)}), bf16[1,32,4,1,256]{4,2,3,0,1:T(4,128)(2,1)S(1)}, u32[]{:S(2)}, u32[]{:S(2)}) async-start(bf16[1,32,4,1,256]{4,2,3,0,1:T(4,128)(2,1)} %bitcast.57), calls=%async_computation.8 | async-start | bytes 131072 | tf_op jit(solution)/shard_map/all_to_all | solution.py:64
  47.1 2.0 gather_fusion.1
  49.2 2.2 reshape.662
  52.3 2.1 gather_fusion.5
  55.6 7.4 %all-to-all-start.2 = ((bf16[1,32,4,1,256]{4,2,3,0,1:T(4,128)(2,1)}), bf16[1,32,4,1,256]{4,2,3,0,1:T(4,128)(2,1)S(1)}, u32[]{:S(2)}, u32[]{:S(2)}) async-start(bf16[1,32,4,1,256]{4,2,3,0,1:T(4,128)(2,1)} %bitcast.18), calls=%async_computation.2 | async-start | bytes 131072 | tf_op jit(solution)/shard_map/all_to_all | solution.py:64
  66.1 2.6 all-to-all-done.2
  68.7 5.6 %all-to-all-start = ((bf16[1,32,4,1,768]{4,2,3,0,1:T(4,128)(2,1)}), bf16[1,32,4,1,768]{4,2,3,0,1:T(4,128)(2,1)S(1)}, u32[]{:S(2)}, u32[]{:S(2)}) async-start(bf16[1,32,4,1,768]{4,2,3,0,1:T(4,128)(2,1)} %bitcast.6), calls=%async_computation | async-start | bytes 393216 | tf_op jit(solution)/shard_map/all_to_all | solution.py:64
  74.3 6.6 %all-to-all-done = bf16[1,32,4,1,768]{4,2,3,0,1:T(4,128)(2,1)S(1)} async-done(((bf16[1,32,4,1,768]{4,2,3,0,1:T(4,128)(2,1)}), bf16[1,32,4,1,768]{4,2,3,0,1:T(4,128)(2,1)S(1)}, u32[]{:S(2)}, u32[]{:S(2)}) %all-to-all-start) | async-done | bytes 196640 | tf_op jit(solution)/shard_map/all_to_all | solution.py:64
  80.9 5.5 %all-to-all-start.3 = ((bf16[1,32,4,1,768]{4,2,3,0,1:T(4,128)(2,1)}), bf16[1,32,4,1,768]{4,2,3,0,1:T(4,128)(2,1)S(1)}, u32[]{:S(2)}, u32[]{:S(2)}) async-start(bf16[1,32,4,1,768]{4,2,3,0,1:T(4,128)(2,1)} %bitcast.28), calls=%async_computation.3 | async-start | bytes 393216 | tf_op jit(solution)/shard_map/all_to_all | solution.py:64
  86.4 6.6 %all-to-all-done.3 = bf16[1,32,4,1,768]{4,2,3,0,1:T(4,128)(2,1)S(1)} async-done(((bf16[1,32,4,1,768]{4,2,3,0,1:T(4,128)(2,1)}), bf16[1,32,4,1,768]{4,2,3,0,1:T(4,128)(2,1)S(1)}, u32[]{:S(2)}, u32[]{:S(2)}) %all-to-all-start.3) | async-done | bytes 196640 | tf_op jit(solution)/shard_map/all_to_all | solution.py:64
  92.9 5.5 %all-to-all-start.12 = ((bf16[1,32,4,1,256]{4,2,3,0,1:T(4,128)(2,1)}), bf16[1,32,4,1,256]{4,2,3,0,1:T(4,128)(2,1)S(1)}, u32[]{:S(2)}, u32[]{:S(2)}) async-start(bf16[1,32,4,1,256]{4,2,3,0,1:T(4,128)(2,1)} %bitcast.76), calls=%async_computation.12 | async-start | bytes 131072 | tf_op jit(solution)/shard_map/all_to_all | solution.py:64
  100.1 4.1 %all-to-all-done.12 = bf16[1,32,4,1,256]{4,2,3,0,1:T(4,128)(2,1)S(1)} async-done(((bf16[1,32,4,1,256]{4,2,3,0,1:T(4,128)(2,1)}), bf16[1,32,4,1,256]{4,2,3,0,1:T(4,128)(2,1)S(1)}, u32[]{:S(2)}, u32[]{:S(2)}) %all-to-all-start.12) | async-done | bytes 65568 | tf_op jit(solution)/shard_map/all_to_all | solution.py:64
  104.1 5.6 %all-to-all-start.5 = ((bf16[1,32,4,1,256]{4,2,3,0,1:T(4,128)(2,1)}), bf16[1,32,4,1,256]{4,2,3,0,1:T(4,128)(2,1)S(1)}, u32[]{:S(2)}, u32[]{:S(2)}) async-start(bf16[1,32,4,1,256]{4,2,3,0,1:T(4,128)(2,1)} %bitcast.40), calls=%async_computation.5 | async-start | bytes 131072 | tf_op jit(solution)/shard_map/all_to_all | solution.py:64
  110.7 4.8 %all-to-all-done.5 = bf16[1,32,4,1,256]{4,2,3,0,1:T(4,128)(2,1)S(1)} async-done(((bf16[1,32,4,1,256]{4,2,3,0,1:T(4,128)(2,1)}), bf16[1,32,4,1,256]{4,2,3,0,1:T(4,128)(2,1)S(1)}, u32[]{:S(2)}, u32[]{:S(2)}) %all-to-all-start.5) | async-done | bytes 65568 | tf_op jit(solution)/shard_map/all_to_all | solution.py:64
  115.5 8.6 %all-to-all-start.1 = ((bf16[1,4,8,4,1,768]{5,3,1,4,0,2:T(4,128)(2,1)}), bf16[1,4,8,4,1,768]{5,3,1,4,0,2:T(4,128)(2,1)}, u32[]{:S(2)}, u32[]{:S(2)}) async-start(bf16[1,4,8,4,1,768]{5,3,1,4,0,2:T(4,128)(2,1)} %get-tuple-element.46), calls=%async_computation.1 | async-start | bytes 393216 | tf_op jit(solution)/shard_map/all_to_all | solution.py:84
  124.7 1.2 and_reduce_fusion.5
  125.9 5.5 %gather_fusion.8 = bf16[1792,256]{1,0:T(8,128)(2,1)S(1)} fusion(bf16[2432,256]{1,0:T(8,128)(2,1)S(1)} %reshape.643, s32[2048]{0:T(1024)S(1)} %pad_clamp_fusion.1), kind=kCustom, calls=%fused_computation.4.clone | custom fusion | bytes 1842176 | tf_op jit(solution)/shard_map/jit(take_along_axis)/gather | solution.py:36
  131.4 2.0 all-to-all-done.1
  133.4 5.2 %all-to-all-start.4 = ((bf16[1,4,8,4,1,768]{5,3,1,4,0,2:T(4,128)(2,1)}), bf16[1,4,8,4,1,768]{5,3,1,4,0,2:T(4,128)(2,1)S(1)}, u32[]{:S(2)}, u32[]{:S(2)}) async-start(bf16[1,4,8,4,1,768]{5,3,1,4,0,2:T(4,128)(2,1)} %get-tuple-element.47), calls=%async_computation.4 | async-start | bytes 393216 | tf_op jit(solution)/shard_map/all_to_all | solution.py:84
  139.6 1.3 reshape_reshape.30
  140.9 6.4 %all-to-all-done.4 = bf16[1,4,8,4,1,768]{5,3,1,4,0,2:T(4,128)(2,1)S(1)} async-done(((bf16[1,4,8,4,1,768]{5,3,1,4,0,2:T(4,128)(2,1)}), bf16[1,4,8,4,1,768]{5,3,1,4,0,2:T(4,128)(2,1)S(1)}, u32[]{:S(2)}, u32[]{:S(2)}) %all-to-all-start.4) | async-done | bytes 196640 | tf_op jit(solution)/shard_map/all_to_all | solution.py:84
  147.4 5.6 %all-to-all-start.6 = ((bf16[1,32,4,1,3584]{4,2,3,0,1:T(4,128)(2,1)}), bf16[1,32,4,1,3584]{4,2,3,0,1:T(4,128)(2,1)S(1)}, u32[]{:S(2)}, u32[]{:S(2)}) async-start(bf16[1,32,4,1,3584]{4,2,3,0,1:T(4,128)(2,1)} %bitcast.45), calls=%async_computation.6 | async-start | bytes 1835008 | tf_op jit(solution)/shard_map/all_to_all | solution.py:64
  153.1 5.5 %gather_fusion.11 = bf16[1792,256]{1,0:T(8,128)(2,1)S(1)} fusion(bf16[2432,256]{1,0:T(8,128)(2,1)S(1)} %reshape.662, s32[2048]{0:T(1024)S(1)} %pad_clamp_fusion), kind=kCustom, calls=%fused_computation.12.clone | custom fusion | bytes 1842176 | tf_op jit(solution)/shard_map/jit(take_along_axis)/gather | solution.py:36
  158.9 1.3 reshape_reshape.32
  160.2 6.2 %all-to-all-done.6 = bf16[1,32,4,1,3584]{4,2,3,0,1:T(4,128)(2,1)S(1)} async-done(((bf16[1,32,4,1,3584]{4,2,3,0,1:T(4,128)(2,1)}), bf16[1,32,4,1,3584]{4,2,3,0,1:T(4,128)(2,1)S(1)}, u32[]{:S(2)}, u32[]{:S(2)}) %all-to-all-start.6) | async-done | bytes 917536 | tf_op jit(solution)/shard_map/all_to_all | solution.py:64
  166.4 6.5 %all-to-all-start.10 = ((bf16[1,32,4,1,3584]{4,2,3,0,1:T(4,128)(2,1)}), bf16[1,32,4,1,3584]{4,2,3,0,1:T(4,128)(2,1)S(1)}, u32[]{:S(2)}, u32[]{:S(2)}) async-start(bf16[1,32,4,1,3584]{4,2,3,0,1:T(4,128)(2,1)} %bitcast.64), calls=%async_computation.10 | async-start | bytes 1835008 | tf_op jit(solution)/shard_map/all_to_all | solution.py:64
  172.9 13.3 %all-to-all-done.10 = bf16[1,32,4,1,3584]{4,2,3,0,1:T(4,128)(2,1)S(1)} async-done(((bf16[1,32,4,1,3584]{4,2,3,0,1:T(4,128)(2,1)}), bf16[1,32,4,1,3584]{4,2,3,0,1:T(4,128)(2,1)S(1)}, u32[]{:S(2)}, u32[]{:S(2)}) %all-to-all-start.10) | async-done | bytes 917536 | tf_op jit(solution)/shard_map/all_to_all | solution.py:64
  187.1 5.5 %all-to-all-start.9 = ((bf16[8,1,4,32,1,256]{5,3,2,4,1,0:T(8,128)(2,1)}), bf16[8,1,4,32,1,256]{5,3,2,4,1,0:T(8,128)(2,1)}, u32[]{:S(2)}, u32[]{:S(2)}) async-start(bf16[8,1,4,32,1,256]{5,3,2,4,1,0:T(8,128)(2,1)} %stack.6), calls=%async_computation.9 | async-start | bytes 1048576 | tf_op jit(solution)/shard_map/all_to_all | solution.py:94
  193.0 1.3 gather_fusion.9
  194.7 1.3 gather_fusion.12
  196.1 13.8 %all-to-all-done.9 = bf16[8,1,4,32,1,256]{5,3,2,4,1,0:T(8,128)(2,1)} async-done(((bf16[8,1,4,32,1,256]{5,3,2,4,1,0:T(8,128)(2,1)}), bf16[8,1,4,32,1,256]{5,3,2,4,1,0:T(8,128)(2,1)}, u32[]{:S(2)}, u32[]{:S(2)}) %all-to-all-start.9) | async-done | bytes 524320 | tf_op jit(solution)/shard_map/all_to_all | solution.py:94
  210.7 5.8 %all-to-all-start.13 = ((bf16[8,1,4,32,1,256]{5,3,2,4,1,0:T(8,128)(2,1)}), bf16[8,1,4,32,1,256]{5,3,2,4,1,0:T(8,128)(2,1)}, u32[]{:S(2)}, u32[]{:S(2)}) async-start(bf16[8,1,4,32,1,256]{5,3,2,4,1,0:T(8,128)(2,1)} %stack.7), calls=%async_computation.13 | async-start | bytes 1048576 | tf_op jit(solution)/shard_map/all_to_all | solution.py:94
  216.5 1.8 fusion.3
  218.3 14.9 %all-to-all-done.13 = bf16[8,1,4,32,1,256]{5,3,2,4,1,0:T(8,128)(2,1)} async-done(((bf16[8,1,4,32,1,256]{5,3,2,4,1,0:T(8,128)(2,1)}), bf16[8,1,4,32,1,256]{5,3,2,4,1,0:T(8,128)(2,1)}, u32[]{:S(2)}, u32[]{:S(2)}) %all-to-all-start.13) | async-done | bytes 524320 | tf_op jit(solution)/shard_map/all_to_all | solution.py:94
  233.2 29.0 %all_to_all.190 = bf16[1,4,8,4,1,3584]{5,3,1,4,0,2:T(4,128)(2,1)S(1)} all-to-all(bf16[1,4,8,4,1,3584]{5,3,1,4,0,2:T(4,128)(2,1)S(1)} %get-tuple-element.44), channel_id=1, replica_groups=mesh['fsdp'=32,'tp'=8] {'tp'}, dimensions={2} | all-to-all | bytes 1835008 | tf_op jit(solution)/shard_map/all_to_all | solution.py:87
  262.2 4.9 %all-to-all-start.11 = ((bf16[1,4,8,4,1,3584]{5,3,1,4,0,2:T(4,128)(2,1)}), bf16[1,4,8,4,1,3584]{5,3,1,4,0,2:T(4,128)(2,1)S(1)}, u32[]{:S(2)}, u32[]{:S(2)}) async-start(bf16[1,4,8,4,1,3584]{5,3,1,4,0,2:T(4,128)(2,1)} %get-tuple-element.45), calls=%async_computation.11 | async-start | bytes 1835008 | tf_op jit(solution)/shard_map/all_to_all | solution.py:87
  267.1 42.6 %all-gather = bf16[1,1,4,32,8,256]{5,3,4,2,1,0:T(8,128)(2,1)S(1)} all-gather(bf16[1,1,4,32,1,256]{5,3,4,2,1,0:T(8,128)(2,1)S(1)} %bitcast.221), channel_id=2, replica_groups=mesh['fsdp'=32,'tp'=8] {'tp'}, dimensions={4}, use_global_device_ids=true | all-gather | bytes 589824 | tf_op jit(solution)/shard_map/all_gather | solution.py:92
  310.2 25.4 %all-gather.1 = bf16[1,1,4,32,8,256]{5,3,4,2,1,0:T(8,128)(2,1)S(1)} all-gather(bf16[1,1,4,32,1,256]{5,3,4,2,1,0:T(8,128)(2,1)S(1)} %bitcast.222), channel_id=3, replica_groups=mesh['fsdp'=32,'tp'=8] {'tp'}, dimensions={4}, use_global_device_ids=true | all-gather | bytes 589824 | tf_op jit(solution)/shard_map/all_gather | solution.py:92
  336.8 1.2 reshape.463
  340.1 1.3 fusion
  341.7 1.3 pad_maximum_fusion.1
  343.0 1.3 copy.110
  345.3 1.3 copy.117
  348.1 1.1 reshape.465
  349.8 1.1 reshape.470
  351.0 2.2 convert_bitcast_fusion
  354.3 3.7 %pad_maximum_fusion = bf16[2,4,896,512]{3,2,1,0:T(8,128)(2,1)} fusion(bf16[1,4,896,512]{3,2,1,0:T(8,128)(2,1)S(1)} %convert_bitcast_fusion, bf16[1,4,896,512]{3,2,1,0:T(8,128)(2,1)S(1)} %convert_bitcast_fusion.1), kind=kLoop, calls=%fused_computation.14 | loop fusion | flops 3670016 | bytes 14680064 | tf_op jit(solution)/shard_map/concatenate | solution.py:123
  (118 shorter events, 30.2 us)
Async XLA Ops:
  0.6 65.3 %copy-start = (s32[32,8]{0,1:T(8,128)S(1)}, s32[32,8]{0,1:T(8,128)}, u32[]{:S(2)}) copy-start(s32[32,8]{0,1:T(8,128)} %param.19) | copy-start | bytes 3076
  35.2 20.4 %all-to-all-start.8 = ((bf16[1,32,4,1,256]{4,2,3,0,1:T(4,128)(2,1)}), bf16[1,32,4,1,256]{4,2,3,0,1:T(4,128)(2,1)S(1)}, u32[]{:S(2)}, u32[]{:S(2)}) async-start(bf16[1,32,4,1,256]{4,2,3,0,1:T(4,128)(2,1)} %bitcast.57), calls=%async_computation.8 | async-start | bytes 131072 | tf_op jit(solution)/shard_map/all_to_all | solution.py:64
  55.6 13.1 %all-to-all-start.2 = ((bf16[1,32,4,1,256]{4,2,3,0,1:T(4,128)(2,1)}), bf16[1,32,4,1,256]{4,2,3,0,1:T(4,128)(2,1)S(1)}, u32[]{:S(2)}, u32[]{:S(2)}) async-start(bf16[1,32,4,1,256]{4,2,3,0,1:T(4,128)(2,1)} %bitcast.18), calls=%async_computation.2 | async-start | bytes 131072 | tf_op jit(solution)/shard_map/all_to_all | solution.py:64
  68.7 12.2 %all-to-all-start = ((bf16[1,32,4,1,768]{4,2,3,0,1:T(4,128)(2,1)}), bf16[1,32,4,1,768]{4,2,3,0,1:T(4,128)(2,1)S(1)}, u32[]{:S(2)}, u32[]{:S(2)}) async-start(bf16[1,32,4,1,768]{4,2,3,0,1:T(4,128)(2,1)} %bitcast.6), calls=%async_computation | async-start | bytes 393216 | tf_op jit(solution)/shard_map/all_to_all | solution.py:64
  74.3 41.2 %copy-start.8 = (pred[8]{0:T(512)(128)(4,1)}, pred[8]{0:T(512)(128)(4,1)S(1)}, u32[]{:S(2)}) copy-start(pred[8]{0:T(512)(128)(4,1)S(1)} %compare_and_fusion) | copy-start | bytes 28
  80.9 12.0 %all-to-all-start.3 = ((bf16[1,32,4,1,768]{4,2,3,0,1:T(4,128)(2,1)}), bf16[1,32,4,1,768]{4,2,3,0,1:T(4,128)(2,1)S(1)}, u32[]{:S(2)}, u32[]{:S(2)}) async-start(bf16[1,32,4,1,768]{4,2,3,0,1:T(4,128)(2,1)} %bitcast.28), calls=%async_computation.3 | async-start | bytes 393216 | tf_op jit(solution)/shard_map/all_to_all | solution.py:64
  92.9 11.2 %all-to-all-start.12 = ((bf16[1,32,4,1,256]{4,2,3,0,1:T(4,128)(2,1)}), bf16[1,32,4,1,256]{4,2,3,0,1:T(4,128)(2,1)S(1)}, u32[]{:S(2)}, u32[]{:S(2)}) async-start(bf16[1,32,4,1,256]{4,2,3,0,1:T(4,128)(2,1)} %bitcast.76), calls=%async_computation.12 | async-start | bytes 131072 | tf_op jit(solution)/shard_map/all_to_all | solution.py:64
  104.1 21.8 %copy-start.4 = (bf16[1,32,4,1,256]{4,2,3,0,1:T(4,128)(2,1)}, bf16[1,32,4,1,256]{4,2,3,0,1:T(4,128)(2,1)S(1)}, u32[]{:S(2)}) copy-start(bf16[1,32,4,1,256]{4,2,3,0,1:T(4,128)(2,1)S(1)} %all-to-all-done.12) | copy-start | bytes 196612
  104.1 11.3 %all-to-all-start.5 = ((bf16[1,32,4,1,256]{4,2,3,0,1:T(4,128)(2,1)}), bf16[1,32,4,1,256]{4,2,3,0,1:T(4,128)(2,1)S(1)}, u32[]{:S(2)}, u32[]{:S(2)}) async-start(bf16[1,32,4,1,256]{4,2,3,0,1:T(4,128)(2,1)} %bitcast.40), calls=%async_computation.5 | async-start | bytes 131072 | tf_op jit(solution)/shard_map/all_to_all | solution.py:64
  115.5 10.5 %copy-start.2 = (bf16[1,32,4,1,256]{4,2,3,0,1:T(4,128)(2,1)}, bf16[1,32,4,1,256]{4,2,3,0,1:T(4,128)(2,1)S(1)}, u32[]{:S(2)}) copy-start(bf16[1,32,4,1,256]{4,2,3,0,1:T(4,128)(2,1)S(1)} %all-to-all-done.5) | copy-start | bytes 196612
  115.5 18.0 %all-to-all-start.1 = ((bf16[1,4,8,4,1,768]{5,3,1,4,0,2:T(4,128)(2,1)}), bf16[1,4,8,4,1,768]{5,3,1,4,0,2:T(4,128)(2,1)}, u32[]{:S(2)}, u32[]{:S(2)}) async-start(bf16[1,4,8,4,1,768]{5,3,1,4,0,2:T(4,128)(2,1)} %get-tuple-element.46), calls=%async_computation.1 | async-start | bytes 393216 | tf_op jit(solution)/shard_map/all_to_all | solution.py:84
  133.4 13.9 %all-to-all-start.4 = ((bf16[1,4,8,4,1,768]{5,3,1,4,0,2:T(4,128)(2,1)}), bf16[1,4,8,4,1,768]{5,3,1,4,0,2:T(4,128)(2,1)S(1)}, u32[]{:S(2)}, u32[]{:S(2)}) async-start(bf16[1,4,8,4,1,768]{5,3,1,4,0,2:T(4,128)(2,1)} %get-tuple-element.47), calls=%async_computation.4 | async-start | bytes 393216 | tf_op jit(solution)/shard_map/all_to_all | solution.py:84
  139.6 13.4 %copy-start.6 = (s32[1,1792,1]{1,2,0:T(1,128)S(1)}, s32[1,1792,1]{1,2,0:T(1,128)}, u32[]{:S(2)}) copy-start(s32[1,1792,1]{1,2,0:T(1,128)} %get-tuple-element.35) | copy-start | bytes 21508
  147.4 19.0 %all-to-all-start.6 = ((bf16[1,32,4,1,3584]{4,2,3,0,1:T(4,128)(2,1)}), bf16[1,32,4,1,3584]{4,2,3,0,1:T(4,128)(2,1)S(1)}, u32[]{:S(2)}, u32[]{:S(2)}) async-start(bf16[1,32,4,1,3584]{4,2,3,0,1:T(4,128)(2,1)} %bitcast.45), calls=%async_computation.6 | async-start | bytes 1835008 | tf_op jit(solution)/shard_map/all_to_all | solution.py:64
  153.1 5.5 %copy-start.7 = (pred[1792]{0:T(1024)(128)(4,1)S(1)}, pred[1792]{0:T(1024)(128)(4,1)}, u32[]{:S(2)}) copy-start(pred[1792]{0:T(1024)(128)(4,1)} %get-tuple-element.34) | copy-start | bytes 5380
  166.4 26.2 %copy-start.5 = (bf16[1,32,4,1,256]{4,2,3,0,1:T(4,128)(2,1)S(1)}, bf16[1,32,4,1,256]{4,2,3,0,1:T(4,128)(2,1)}, u32[]{:S(2)}) copy-start(bf16[1,32,4,1,256]{4,2,3,0,1:T(4,128)(2,1)} %copy-done.4) | copy-start | bytes 196612
  166.4 19.9 %all-to-all-start.10 = ((bf16[1,32,4,1,3584]{4,2,3,0,1:T(4,128)(2,1)}), bf16[1,32,4,1,3584]{4,2,3,0,1:T(4,128)(2,1)S(1)}, u32[]{:S(2)}, u32[]{:S(2)}) async-start(bf16[1,32,4,1,3584]{4,2,3,0,1:T(4,128)(2,1)} %bitcast.64), calls=%async_computation.10 | async-start | bytes 1835008 | tf_op jit(solution)/shard_map/all_to_all | solution.py:64
  187.1 22.7 %all-to-all-start.9 = ((bf16[8,1,4,32,1,256]{5,3,2,4,1,0:T(8,128)(2,1)}), bf16[8,1,4,32,1,256]{5,3,2,4,1,0:T(8,128)(2,1)}, u32[]{:S(2)}, u32[]{:S(2)}) async-start(bf16[8,1,4,32,1,256]{5,3,2,4,1,0:T(8,128)(2,1)} %stack.6), calls=%async_computation.9 | async-start | bytes 1048576 | tf_op jit(solution)/shard_map/all_to_all | solution.py:94
  194.7 21.8 %copy-start.9 = (pred[8]{0:T(512)(128)(4,1)S(1)}, pred[8]{0:T(512)(128)(4,1)}, u32[]{:S(2)}) copy-start(pred[8]{0:T(512)(128)(4,1)} %copy-done.8) | copy-start | bytes 28
  210.7 22.5 %all-to-all-start.13 = ((bf16[8,1,4,32,1,256]{5,3,2,4,1,0:T(8,128)(2,1)}), bf16[8,1,4,32,1,256]{5,3,2,4,1,0:T(8,128)(2,1)}, u32[]{:S(2)}, u32[]{:S(2)}) async-start(bf16[8,1,4,32,1,256]{5,3,2,4,1,0:T(8,128)(2,1)} %stack.7), calls=%async_computation.13 | async-start | bytes 1048576 | tf_op jit(solution)/shard_map/all_to_all | solution.py:94
  262.2 87.1 %all-to-all-start.11 = ((bf16[1,4,8,4,1,3584]{5,3,1,4,0,2:T(4,128)(2,1)}), bf16[1,4,8,4,1,3584]{5,3,1,4,0,2:T(4,128)(2,1)S(1)}, u32[]{:S(2)}, u32[]{:S(2)}) async-start(bf16[1,4,8,4,1,3584]{5,3,1,4,0,2:T(4,128)(2,1)} %get-tuple-element.45), calls=%async_computation.11 | async-start | bytes 1835008 | tf_op jit(solution)/shard_map/all_to_all | solution.py:87
  267.1 43.1 %copy-start.3 = (bf16[1,32,4,1,256]{4,2,3,0,1:T(4,128)(2,1)S(1)}, bf16[1,32,4,1,256]{4,2,3,0,1:T(4,128)(2,1)}, u32[]{:S(2)}) copy-start(bf16[1,32,4,1,256]{4,2,3,0,1:T(4,128)(2,1)} %copy-done.2) | copy-start | bytes 196612
  351.0 2.2 copy-start.1
